TPU v7x, 32 devices: a whole 2x2x4 slice. The times are simulated.
32 devices in a mesh: dp: 8 (over y, x, core), seq: 4 (over z).
Axes of the slice: x: 2, y: 2, z: 4, core: 2. Of those that a mesh axis runs over, the one named last changes fastest.
Arguments:
- tokens: bfloat16 [32, 1024, 768], P('dp', 'seq'), may hold values from -6 to 6
- cotangent: bfloat16 [32, 1024, 768], P('dp', 'seq'), may hold values from -6 to 6
- segments: int32 [32, 1024], P('dp'), may hold values from 0 to 4, as said below
- keep_flags: int32 [32, 8], P('dp'), may hold values 0 or 1
- first_gain: float32 [768], P('dp'), may hold values from 0.5 to 1.5
- first_shift: float32 [768], P('dp'), may hold values from -1.2 to 1.2
- joint_weight: float32 [768, 2304], P('dp'), may hold values from -0.21875 to 0.21875
- joint_bias: float32 [1536], P('dp'), may hold values from -1.2 to 1.2
- output_weight: float32 [768, 768], P('dp'), may hold values from -3 to 3
- output_bias: float32 [768], P('dp'), may hold values from -1.2 to 1.2
- second_gain: float32 [768], P('dp'), may hold values from 0.5 to 1.5
- second_shift: float32 [768], P('dp'), may hold values from -1.2 to 1.2
- expand_weight: float32 [768, 3072], P('dp'), may hold values from -0.21875 to 0.21875
- expand_bias: float32 [3072], P('dp'), may hold values from -1.2 to 1.2
- reduce_weight: float32 [3072, 768], P('dp'), may hold values from -0.109375 to 0.109375
- reduce_bias: float32 [768], P('dp'), may hold values from -1.2 to 1.2
Outputs:
- output: bfloat16 [32, 1024, 768], P('dp', 'seq')
- grad_tokens: float32 [32, 1024, 768], P('dp', 'seq')
- first_gain_grad: float32 [768], P('dp')
- first_shift_grad: float32 [768], P('dp')
- joint_weight_grad: float32 [768, 2304], P('dp')
- joint_bias_grad: float32 [1536], P('dp')
- output_weight_grad: float32 [768, 768], P('dp')
- output_bias_grad: float32 [768], P('dp')
- second_gain_grad: float32 [768], P('dp')
- second_shift_grad: float32 [768], P('dp')
- expand_weight_grad: float32 [768, 3072], P('dp')
- expand_bias_grad: float32 [3072], P('dp')
- reduce_weight_grad: float32 [3072, 768], P('dp')
- reduce_bias_grad: float32 [768], P('dp')
Inputs may be any that keep to these rules, and one draw needn't show every extreme that they name: `segments`: positions 0 to 7 of each row hold image p // 2 (class token at even p, distillation token at odd p); then the patch tokens of images 0 to 3 follow in this order, each image's patches contiguous and one or more; the rest of the row, never empty, is padding with the value 4. `keep_flags`: column i < 4 keeps the attention branch of image i, column 4 + i its feed-forward branch.
All inputs are finite; a program needn't handle non-finite values. No bound on the sum of `keep_flags` on one device may be relied on, other than what follows from the above.
Results may differ from a plain program's by a relative error of at most 0.012.
The roundings to bfloat16 on the way count: a program that leaves them out, or rounds other values in their place, can miss the bound.
Values may be sent and summed in bfloat16 or wider, within the bound.
No kernel may reach another device: no remote copies, remote signals or barrier semaphores. Data moves between devices by JAX's collectives and lax.ppermute only.
A program may use at most 192 MiB of HBM per device.

v0:
```python
import jax
import jax.numpy as jnp
from jax import lax
from jax.sharding import PartitionSpec as P

HEADS = 12
HEAD = 64
keep_ratio_inverse = 1.0 / 0.9
score_factor = 0.125
norm_epsilon = 1e-06


def normalize(inputs, gain, shift_b):
    centre = inputs - jnp.mean(inputs, axis=-1, keepdims=True)
    spread = jnp.mean(centre * centre, axis=-1, keepdims=True)
    return centre * lax.rsqrt(spread + norm_epsilon) * gain + shift_b


def gelu_exact(inputs):
    return jax.nn.gelu(inputs, approximate=False)


def matmul(left, right):
    return jnp.dot(left, right, preferred_element_type=jnp.float32)


def left_grad(inputs, grads):
    return lax.dot_general(
        inputs, grads, (((0,), (0,)), ((), ())), preferred_element_type=jnp.float32
    )


def right_grad(grads, weight):
    return lax.dot_general(
        grads, weight, (((1,), (1,)), ((), ())), preferred_element_type=jnp.float32
    )


def row_scores(queries, key_rows, seg_query, seg_key):
    raw_scores = (
        jnp.einsum("shd,lhd->hsl", queries, key_rows, preferred_element_type=jnp.float32)
        * score_factor
    )
    allowed = seg_query[:, None] == seg_key[None, :]
    return jnp.where(allowed[None, :, :], raw_scores, -1e30)


def row_forward(row_data):
    queries, key_rows, value_rows, seg_query, seg_key = row_data
    scores = row_scores(queries, key_rows, seg_query, seg_key)
    row_max = jnp.max(scores, axis=-1, keepdims=True)
    row_sum = jnp.sum(jnp.exp(scores - row_max), axis=-1, keepdims=True)
    log_total = row_max + jnp.log(row_sum)
    attention = jnp.exp(scores - log_total).astype(jnp.bfloat16)
    mixed_rows = jnp.einsum(
        "hsl,lhd->shd", attention, value_rows, preferred_element_type=jnp.float32
    )
    return (mixed_rows.astype(jnp.bfloat16), log_total)


def row_backward(row_data):
    queries, key_rows, value_rows, seg_query, seg_key, log_total, grad_mixed = row_data
    scores = row_scores(queries, key_rows, seg_query, seg_key)
    attention = jnp.exp(scores - log_total)
    grad_attention = jnp.einsum(
        "shd,lhd->hsl", grad_mixed, value_rows, preferred_element_type=jnp.float32
    )
    centre = jnp.sum(attention * grad_attention, axis=-1, keepdims=True)
    grad_scores = (attention * (grad_attention - centre)).astype(jnp.bfloat16)
    grad_queries = (
        jnp.einsum("hsl,lhd->shd", grad_scores, key_rows, preferred_element_type=jnp.float32)
        * score_factor
    )
    grad_keys = (
        jnp.einsum("hsl,shd->lhd", grad_scores, queries, preferred_element_type=jnp.float32)
        * score_factor
    )
    grad_values = jnp.einsum(
        "hsl,shd->lhd",
        attention.astype(jnp.bfloat16),
        grad_mixed,
        preferred_element_type=jnp.float32,
    )
    return (grad_queries, grad_keys, grad_values)


def shards(
    tokens,
    cotangent,
    segments,
    keep_flags,
    first_gain,
    first_shift,
    joint_weight,
    joint_bias,
    output_weight,
    output_bias,
    second_gain,
    second_shift,
    expand_weight,
    expand_bias,
    reduce_weight,
    reduce_bias,
):
    row_count, shard_len, features = tokens.shape
    row_len = segments.shape[1]
    images = keep_flags.shape[1] // 2
    token_count = row_count * shard_len
    offset_seq = lax.axis_index("seq") * shard_len
    seg_local = lax.dynamic_slice_in_dim(segments, offset_seq, shard_len, 1)
    labels = lax.broadcasted_iota(jnp.int32, (1, 1, images), 2)
    onehot = (seg_local[:, :, None] == labels).astype(jnp.float32)
    flags = keep_flags.astype(jnp.float32)
    attn_scale = (jnp.sum(onehot * flags[:, None, :images], axis=-1) * keep_ratio_inverse).reshape(
        token_count, 1
    )
    mlp_scale = (jnp.sum(onehot * flags[:, None, images:], axis=-1) * keep_ratio_inverse).reshape(
        token_count, 1
    )
    gain_a, shift_a, weight_qkv, bias_qv, weight_out, bias_out = (
        lax.all_gather(first_gain.astype(jnp.bfloat16), "dp", axis=0, tiled=True),
        lax.all_gather(first_shift.astype(jnp.bfloat16), "dp", axis=0, tiled=True),
        lax.all_gather(joint_weight.astype(jnp.bfloat16), "dp", axis=0, tiled=True),
        lax.all_gather(joint_bias.astype(jnp.bfloat16), "dp", axis=0, tiled=True),
        lax.all_gather(output_weight.astype(jnp.bfloat16), "dp", axis=0, tiled=True),
        lax.all_gather(output_bias.astype(jnp.bfloat16), "dp", axis=0, tiled=True),
    )
    flat_in = tokens.astype(jnp.float32).reshape(token_count, features)
    normed_a = normalize(flat_in, gain_a.astype(jnp.float32), shift_a.astype(jnp.float32)).astype(
        jnp.bfloat16
    )
    bias_full = jnp.concatenate(
        [
            bias_qv[:features].astype(jnp.float32),
            jnp.zeros((features,), jnp.float32),
            bias_qv[features:].astype(jnp.float32),
        ]
    )
    projected = (matmul(normed_a, weight_qkv) + bias_full).astype(jnp.bfloat16)
    queries = projected[:, :features].reshape(row_count, shard_len, HEADS, HEAD)
    key_local = projected[:, features : 2 * features].reshape(row_count, shard_len, features)
    value_local = projected[:, 2 * features :].reshape(row_count, shard_len, features)
    key_rows, value_rows = (
        lax.all_gather(key_local, "seq", axis=1, tiled=True),
        lax.all_gather(value_local, "seq", axis=1, tiled=True),
    )
    key_heads = key_rows.reshape(row_count, row_len, HEADS, HEAD)
    value_heads = value_rows.reshape(row_count, row_len, HEADS, HEAD)
    mixed_heads, log_total = lax.map(
        row_forward, (queries, key_heads, value_heads, seg_local, segments)
    )
    mixed_flat = mixed_heads.reshape(token_count, features)
    branch_a = matmul(mixed_flat, weight_out) + bias_out.astype(jnp.float32)
    middle = flat_in + attn_scale * branch_a
    gain_b, shift_bb, weight_up, bias_up, weight_down, bias_down = (
        lax.all_gather(second_gain.astype(jnp.bfloat16), "dp", axis=0, tiled=True),
        lax.all_gather(second_shift.astype(jnp.bfloat16), "dp", axis=0, tiled=True),
        lax.all_gather(expand_weight.astype(jnp.bfloat16), "dp", axis=0, tiled=True),
        lax.all_gather(expand_bias.astype(jnp.bfloat16), "dp", axis=0, tiled=True),
        lax.all_gather(reduce_weight.astype(jnp.bfloat16), "dp", axis=0, tiled=True),
        lax.all_gather(reduce_bias.astype(jnp.bfloat16), "dp", axis=0, tiled=True),
    )
    normed_b = normalize(middle, gain_b.astype(jnp.float32), shift_bb.astype(jnp.float32)).astype(
        jnp.bfloat16
    )
    pre_act = matmul(normed_b, weight_up) + bias_up.astype(jnp.float32)
    activated = gelu_exact(pre_act).astype(jnp.bfloat16)
    branch_b = matmul(activated, weight_down) + bias_down.astype(jnp.float32)
    output = (
        (middle + mlp_scale * branch_b).astype(jnp.bfloat16).reshape(row_count, shard_len, features)
    )
    grad_out = cotangent.astype(jnp.float32).reshape(token_count, features)
    grad_branch_b = (mlp_scale * grad_out).astype(jnp.bfloat16)
    g_reduce_weight = left_grad(activated, grad_branch_b)
    g_reduce_bias = jnp.sum(grad_branch_b, axis=0, dtype=jnp.float32)
    grad_activated = right_grad(grad_branch_b, weight_down)
    gelu_value, gelu_pull = jax.vjp(gelu_exact, pre_act)
    grad_pre = gelu_pull(grad_activated)[0].astype(jnp.bfloat16)
    g_expand_weight = left_grad(normed_b, grad_pre)
    g_expand_bias = jnp.sum(grad_pre, axis=0, dtype=jnp.float32)
    grad_normed_b = right_grad(grad_pre, weight_up)
    norm_value_b, norm_pull_b = jax.vjp(
        normalize, middle, gain_b.astype(jnp.float32), shift_bb.astype(jnp.float32)
    )
    grad_middle_norm, g_second_gain, g_second_shift = norm_pull_b(grad_normed_b)
    grad_middle = grad_out + grad_middle_norm
    grad_branch_a = (attn_scale * grad_middle).astype(jnp.bfloat16)
    g_output_weight = left_grad(mixed_flat, grad_branch_a)
    g_output_bias = jnp.sum(grad_branch_a, axis=0, dtype=jnp.float32)
    grad_mixed = (
        right_grad(grad_branch_a, weight_out)
        .astype(jnp.bfloat16)
        .reshape(row_count, shard_len, HEADS, HEAD)
    )
    grad_queries, grad_key_rows, grad_value_rows = lax.map(
        row_backward, (queries, key_heads, value_heads, seg_local, segments, log_total, grad_mixed)
    )
    key_sum, value_sum = (
        lax.psum_scatter(
            grad_key_rows.reshape(row_count, row_len, features),
            "seq",
            scatter_dimension=1,
            tiled=True,
        ),
        lax.psum_scatter(
            grad_value_rows.reshape(row_count, row_len, features),
            "seq",
            scatter_dimension=1,
            tiled=True,
        ),
    )
    grad_projected = jnp.concatenate(
        [
            grad_queries.reshape(token_count, features),
            key_sum.reshape(token_count, features),
            value_sum.reshape(token_count, features),
        ],
        axis=1,
    ).astype(jnp.bfloat16)
    g_joint_weight = left_grad(normed_a, grad_projected)
    column_sums = jnp.sum(grad_projected, axis=0, dtype=jnp.float32)
    g_joint_bias = jnp.concatenate([column_sums[:features], column_sums[2 * features :]])
    grad_normed_a = right_grad(grad_projected, weight_qkv)
    norm_value_a, norm_pull_a = jax.vjp(
        normalize, flat_in, gain_a.astype(jnp.float32), shift_a.astype(jnp.float32)
    )
    grad_in_norm, g_first_gain, g_first_shift = norm_pull_a(grad_normed_a)
    grad_tokens = (grad_middle + grad_in_norm).reshape(row_count, shard_len, features)
    every_shard = (
        lax.psum_scatter(g_first_gain, "dp", scatter_dimension=0, tiled=True),
        lax.psum_scatter(g_first_shift, "dp", scatter_dimension=0, tiled=True),
        lax.psum_scatter(g_joint_weight, "dp", scatter_dimension=0, tiled=True),
        lax.psum_scatter(g_joint_bias, "dp", scatter_dimension=0, tiled=True),
        lax.psum_scatter(g_output_weight, "dp", scatter_dimension=0, tiled=True),
        lax.psum_scatter(g_output_bias, "dp", scatter_dimension=0, tiled=True),
        lax.psum_scatter(g_second_gain, "dp", scatter_dimension=0, tiled=True),
        lax.psum_scatter(g_second_shift, "dp", scatter_dimension=0, tiled=True),
        lax.psum_scatter(g_expand_weight, "dp", scatter_dimension=0, tiled=True),
        lax.psum_scatter(g_expand_bias, "dp", scatter_dimension=0, tiled=True),
        lax.psum_scatter(g_reduce_weight, "dp", scatter_dimension=0, tiled=True),
        lax.psum_scatter(g_reduce_bias, "dp", scatter_dimension=0, tiled=True),
    )
    (
        s_first_gain,
        s_first_shift,
        s_joint_weight,
        s_joint_bias,
        s_output_weight,
        s_output_bias,
        s_second_gain,
        s_second_shift,
        s_expand_weight,
        s_expand_bias,
        s_reduce_weight,
        s_reduce_bias,
    ) = lax.psum(
        (
            every_shard[0],
            every_shard[1],
            every_shard[2],
            every_shard[3],
            every_shard[4],
            every_shard[5],
            every_shard[6],
            every_shard[7],
            every_shard[8],
            every_shard[9],
            every_shard[10],
            every_shard[11],
        ),
        "seq",
    )
    return (
        output,
        grad_tokens,
        s_first_gain,
        s_first_shift,
        s_joint_weight,
        s_joint_bias,
        s_output_weight,
        s_output_bias,
        s_second_gain,
        s_second_shift,
        s_expand_weight,
        s_expand_bias,
        s_reduce_weight,
        s_reduce_bias,
    )


def solution(mesh):
    return jax.shard_map(
        shards,
        mesh=mesh,
        in_specs=(
            P("dp", "seq", None),
            P("dp", "seq", None),
            P("dp", None),
            P("dp", None),
            P("dp"),
            P("dp"),
            P("dp", None),
            P("dp"),
            P("dp", None),
            P("dp"),
            P("dp"),
            P("dp"),
            P("dp", None),
            P("dp"),
            P("dp", None),
            P("dp"),
        ),
        out_specs=(
            P("dp", "seq", None),
            P("dp", "seq", None),
            P("dp"),
            P("dp"),
            P("dp", None),
            P("dp"),
            P("dp", None),
            P("dp"),
            P("dp"),
            P("dp"),
            P("dp", None),
            P("dp"),
            P("dp", None),
            P("dp"),
        ),
        check_vma=False,
    )
```

profile of v0, /device:TPU:0, one launch (start us, length us, event | category | flops | bytes accessed | tf_op | source)
XLA Modules:
  0.0 1413.1 jit_solution(12734546401829602809)
XLA Ops:
  18.1 27.3 %all-reduce.18 = (bf16[768]{0:T(1024)(128)(2,1)S(1)}, bf16[768]{0:T(1024)(128)(2,1)S(1)}, bf16[1536]{0:T(1024)(128)(2,1)S(1)}, bf16[768]{0:T(1024)(128)(2,1)S(1)...) all-reduce(bf16[768]{0:T(1024)(128)(2,1)S(1)} %dynamic-update-slice, ...), channel_id=1, replica_groups=mesh['dp'=8,'seq'=4] {'dp'}, use_global_device_ids=true, to_apply=%add.1 | all-reduce | flops 6144 | bytes 24576
  80.0 92.8 %all-gather.12.cloned.1.call-done = bf16[4,1024,768]{2,1,0:T(8,128)(2,1)} async-done(((bf16[4,256,768]{2,1,0:T(8,128)(2,1)}), bf16[4,1024,768]{2,1,0:T(8,128)(2,1)}) %all-gather.12.cloned.1.call-update) | async-done | bytes 6291472 | tf_op jit(solution)/shard_map/all_gather | solution.py:144
  181.5 106.4 %all-gather.10.cloned.1.call-done = bf16[4,1024,768]{2,1,0:T(8,128)(2,1)} async-done(((bf16[4,256,768]{2,1,0:T(8,128)(2,1)}), bf16[4,1024,768]{2,1,0:T(8,128)(2,1)}) %all-gather.10.cloned.1.call-update) | async-done | bytes 6291472 | tf_op jit(solution)/shard_map/all_gather | solution.py:145
  296.6 53.3 %while.26 = (s32[]{:T(128)}, bf16[4,256,12,64]{1,3,2,0:T(8,128)(2,1)}, f32[4,12,256,1]{2,1,3,0:T(8,128)S(1)}, bf16[4,1024,12,64]{1,3,2,0:T(8,128)(2,1)}, s32[4,2...) while((s32[]{:T(128)}, ...), condition=%wide.region_6.7_spmd, body=%wide.region_3.6_spmd.sunk | while | flops 840365056 | bytes 42861680 | solution.py:149
  359.8 38.3 %multiply_convert_fusion.1 = (bf16[1024,3072]{1,0:T(8,128)(2,1)}, f32[1024,3072]{1,0:T(8,128)}, f32[1024,3072]{1,0:T(8,128)}) fusion(f32[3072]{0:T(1024)S(1)} %bitcast.248, bf16[768,3072]{1,0:T(8,128)(2,1)} %all-gather.16.cloned.1.call-done, f32[1024,768]{1,0:T(8,128)} %copy-done.2, f32[768]{0:T(1024)S(1)} %convert_element_type.152, ...), kind=kOutput, calls=%fused_computation.68 | convolution fusion | flops 5043388416 | bytes 39348224 | tf_op jit(solution)/shard_map/dot_general | solution.py:24
  398.2 17.4 %convert_reduce_fusion = (f32[3072]{0:T(1024)}, bf16[1024,3072]{1,0:T(8,128)(2,1)}) fusion(f32[1024,3072]{1,0:T(8,128)} %get-tuple-element.297, bf16[1024,768]{1,0:T(8,128)(2,1)S(1)} %copy-done.14, bf16[3072,768]{1,0:T(8,128)(2,1)} %all-gather.18.cloned.1.call-done, f32[1024,3072]{1,0:T(8,128)} %get-tuple-element.319, f32[3072]{0:T(1024)S(1)} %bitcast.249), kind=kOutput, calls=%fused_computation.66 | convolution fusion | flops 4885312512 | bytes 37773312 | tf_op jit(solution)/shard_map/dot_general | solution.py:34
  415.6 10.2 multiply_reduce_fusion.1
  439.8 120.7 %while.27 = (s32[]{:T(128)}, bf16[4,256,12,64]{1,3,2,0:T(8,128)(2,1)}, f32[4,1024,12,64]{1,3,2,0:T(8,128)}, f32[4,1024,12,64]{1,3,2,0:T(8,128)}, bf16[4,1024,12,...) while((s32[]{:T(128)}, ...), condition=%wide.region_14.15_spmd, body=%wide.region_12.14_spmd.sunk | while | flops 2061693952 | bytes 121487552 | solution.py:195
  448.0 8.8 multiply_reduce_fusion.5
  478.1 8.8 multiply_reduce_fusion.5
  538.5 8.8 multiply_reduce_fusion.5
  566.3 10.8 fusion.87
  577.2 9.9 fusion.98
  591.3 179.2 %reduce-scatter.9.cloned.1.call-done = f32[4,256,768]{1,2,0:T(8,128)} async-done(((f32[4,1024,768]{1,2,0:T(8,128)}), f32[4,256,768]{1,2,0:T(8,128)}) %reduce-scatter.9.cloned.1.call-update) | async-done | bytes 3145744 | tf_op jit(solution)/shard_map/reduce_scatter | solution.py:205
  778.8 206.9 %reduce-scatter.7.cloned.1.call-done = f32[4,256,768]{1,2,0:T(8,128)} async-done(((f32[4,1024,768]{1,2,0:T(8,128)}), f32[4,256,768]{1,2,0:T(8,128)}) %reduce-scatter.7.cloned.1.call-update) | async-done | bytes 3145744 | tf_op jit(solution)/shard_map/reduce_scatter | solution.py:199
  994.1 9.8 fusion.84
  1007.8 24.8 %reduce-scatter.13.cloned.1.call-done = f32[96,768]{1,0:T(8,128)} async-done(((f32[768,768]{1,0:T(8,128)}), f32[96,768]{1,0:T(8,128)}) %reduce-scatter.13.cloned.1.call-update) | async-done | bytes 294928 | tf_op jit(solution)/shard_map/reduce_scatter | solution.py:234
  1032.5 80.2 %reduce-scatter.15.cloned.1.call-done = f32[96,3072]{1,0:T(8,128)} async-done(((f32[768,3072]{1,0:T(8,128)}), f32[96,3072]{1,0:T(8,128)}) %reduce-scatter.15.cloned.1.call-update) | async-done | bytes 1179664 | tf_op jit(solution)/shard_map/reduce_scatter | solution.py:238
  1112.8 80.4 %reduce-scatter.17.cloned.1.call-done = f32[384,768]{1,0:T(8,128)} async-done(((f32[3072,768]{1,0:T(8,128)}), f32[384,768]{1,0:T(8,128)}) %reduce-scatter.17.cloned.1.call-update) | async-done | bytes 1179664 | tf_op jit(solution)/shard_map/reduce_scatter | solution.py:240
  1193.1 68.9 %reduce-scatter.11.cloned.1.call-done = f32[96,2304]{1,0:T(8,128)} async-done(((f32[768,2304]{1,0:T(8,128)}), f32[96,2304]{1,0:T(8,128)}) %reduce-scatter.11.cloned.1.call-update) | async-done | bytes 884752 | tf_op jit(solution)/shard_map/reduce_scatter | solution.py:232
  1262.1 9.8 add_convert_fusion.2
  1281.1 25.1 %all-reduce.15 = (f32[768]{0:T(1024)S(1)}, f32[768]{0:T(1024)S(1)}, f32[1536]{0:T(1024)S(1)}, f32[768]{0:T(1024)S(1)}, f32[768]{0:T(1024)S(1)}, /*index=5*/f32[7...) all-reduce(f32[768]{0:T(1024)S(1)} %get-tuple-element.218, ...), channel_id=4, replica_groups=mesh['dp'=8,'seq'=4] {'dp'}, use_global_device_ids=true, to_apply=%region_20.21.clone | all-reduce | flops 9216 | bytes 73728
  1306.9 13.4 all-reduce.16
  1325.0 74.0 %all-reduce.21.cloned.1.call-done = (f32[96,2304]{1,0:T(8,128)}, f32[96,768]{1,0:T(8,128)}, f32[96,3072]{1,0:T(8,128)}, f32[384,768]{1,0:T(8,128)}) async-done(((f32[96,2304]{1,0:T(8,128)}, f32[96,768]{1,0:T(8,128)}, f32[96,3072]{1,0:T(8,128)}, f32[384,768]{1,0:T(8,128)}), (f32[96,2304]{1,0:T(8,128)}, f32[96,768]{1,0:T(8,128)}, f32[96,3072]{1,0:T(8,128)}, ...) | async-done | bytes 3538960 | tf_op jit(solution)/shard_map/psum | solution.py:256
  (321 shorter events, 282.5 us)
Async XLA Ops:
  7.2 39.9 %copy-start = (bf16[4,256,768]{2,1,0:T(8,128)(2,1)S(1)}, bf16[4,256,768]{2,1,0:T(8,128)(2,1)}, u32[]{:S(2)}) copy-start(bf16[4,256,768]{2,1,0:T(8,128)(2,1)} %param.20) | copy-start | bytes 4718596
  7.2 41.8 %all-gather.8.cloned.1.call-start = ((), (), s32[]{:S(2)}) async-start(), calls=%async_computation.6 | async-start | bytes 3981312 | tf_op jit(solution)/shard_map/all_gather | solution.py:123
  9.3 163.4 %all-gather.12.cloned.1.call-start = ((), (), s32[]{:S(2)}) async-start(), calls=%async_computation.8 | async-start | bytes 7864320 | tf_op jit(solution)/shard_map/all_gather | solution.py:144
  57.9 230.0 %all-gather.10.cloned.1.call-start = ((), (), s32[]{:S(2)}) async-start(), calls=%async_computation.7 | async-start | bytes 7864320 | tf_op jit(solution)/shard_map/all_gather | solution.py:145
  58.0 14.8 %copy-start.6 = (bf16[4,256,768]{2,1,0:T(8,128)(2,1)S(1)}, bf16[4,256,768]{2,1,0:T(8,128)(2,1)}, u32[]{:S(2)}) copy-start(bf16[4,256,768]{2,1,0:T(8,128)(2,1)} %param.21) | copy-start | bytes 4718596
  58.7 295.4 %all-gather.14.cloned.1.call-start = ((), (), s32[]{:S(2)}) async-start(), calls=%async_computation.9 | async-start | bytes 1327104 | tf_op jit(solution)/shard_map/all_gather | solution.py:125
  59.4 300.4 %all-gather.16.cloned.1.call-start = ((), (), s32[]{:S(2)}) async-start(), calls=%async_computation.10 | async-start | bytes 5308416 | tf_op jit(solution)/shard_map/all_gather | solution.py:158
  61.6 336.5 %all-gather.18.cloned.1.call-start = ((), (), s32[]{:S(2)}) async-start(), calls=%async_computation.11 | async-start | bytes 5308416 | tf_op jit(solution)/shard_map/all_gather | solution.py:160
  63.9 706.6 %reduce-scatter.9.cloned.1.call-start = ((), (), s32[]{:S(2)}) async-start(), calls=%async_computation.13 | async-start | bytes 15728640 | tf_op jit(solution)/shard_map/reduce_scatter | solution.py:205
  64.1 361.7 %copy-start.25 = (f32[768]{0:T(1024)}, f32[768]{0:T(1024)S(1)}, u32[]{:S(2)}) copy-start(f32[768]{0:T(1024)S(1)} %convert_element_type.150) | copy-start | bytes 9220
  64.1 295.7 %copy-start.33 = (f32[768]{0:T(1024)}, f32[768]{0:T(1024)S(1)}, u32[]{:S(2)}) copy-start(f32[768]{0:T(1024)S(1)} %convert_element_type.152) | copy-start | bytes 9220
  357.6 68.2 %copy-start.19 = (f32[1024]{0:T(1024)}, f32[1024]{0:T(1024)S(1)}, u32[]{:S(2)}) copy-start(f32[1024]{0:T(1024)S(1)} %broadcast_multiply_fusion) | copy-start | bytes 12292
  359.8 66.0 %copy-start.22 = (f32[1024]{0:T(1024)}, f32[1024]{0:T(1024)S(1)}, u32[]{:S(2)}) copy-start(f32[1024]{0:T(1024)S(1)} %fusion.81) | copy-start | bytes 12292
  359.8 38.3 %copy-start.14 = (bf16[1024,768]{1,0:T(8,128)(2,1)S(1)}, bf16[1024,768]{1,0:T(8,128)(2,1)}, u32[]{:S(2)}) copy-start(bf16[1024,768]{1,0:T(8,128)(2,1)} %fusion.69) | copy-start | bytes 4718596
  398.2 17.5 %copy-start.3 = (f32[1024,768]{1,0:T(8,128)S(1)}, f32[1024,768]{1,0:T(8,128)}, u32[]{:S(2)}) copy-start(f32[1024,768]{1,0:T(8,128)} %copy-done.2) | copy-start | bytes 9437188
  560.5 425.3 %reduce-scatter.7.cloned.1.call-start = ((), (), s32[]{:S(2)}) async-start(), calls=%async_computation.12 | async-start | bytes 15728640 | tf_op jit(solution)/shard_map/reduce_scatter | solution.py:199
  561.3 471.2 %reduce-scatter.13.cloned.1.call-start = ((), (), s32[]{:S(2)}) async-start(), calls=%async_computation.15 | async-start | bytes 2654208 | tf_op jit(solution)/shard_map/reduce_scatter | solution.py:234
  566.2 546.5 %reduce-scatter.15.cloned.1.call-start = ((), (), s32[]{:S(2)}) async-start(), calls=%async_computation.16 | async-start | bytes 10616832 | tf_op jit(solution)/shard_map/reduce_scatter | solution.py:238
  577.1 616.0 %reduce-scatter.17.cloned.1.call-start = ((), (), s32[]{:S(2)}) async-start(), calls=%async_computation.17 | async-start | bytes 10616832 | tf_op jit(solution)/shard_map/reduce_scatter | solution.py:240
  587.1 674.9 %reduce-scatter.11.cloned.1.call-start = ((), (), s32[]{:S(2)}) async-start(), calls=%async_computation.14 | async-start | bytes 7962624 | tf_op jit(solution)/shard_map/reduce_scatter | solution.py:232
  1003.9 258.1 %copy-start.41 = (f32[1,2,4,128]{3,1,2,0:T(2,128)S(1)}, f32[1,2,4,128]{3,1,2,0:T(2,128)}, u32[]{:S(2)}) copy-start(f32[1,2,4,128]{3,1,2,0:T(2,128)} %copy-done.40) | copy-start | bytes 12292
  1003.9 395.1 %all-reduce.21.cloned.1.call-start = ((), (), s32[]{:S(2)}) async-start(), calls=%async_computation.18 | async-start | bytes 7077888 | tf_op jit(solution)/shard_map/psum | solution.py:256
  1277.9 42.4 %copy-start.8 = (bf16[4,256,768]{2,1,0:T(8,128)(2,1)S(1)}, bf16[4,256,768]{2,1,0:T(8,128)(2,1)}, u32[]{:S(2)}) copy-start(bf16[4,256,768]{2,1,0:T(8,128)(2,1)} %param.21) | copy-start | bytes 4718596
  1277.9 42.4 %copy-start.38 = (f32[1024]{0:T(1024)S(1)}, f32[1024]{0:T(1024)}, u32[]{:S(2)}) copy-start(f32[1024]{0:T(1024)} %copy-done.37) | copy-start | bytes 12292
  (46 other events, 209.2 us)
Sparse Core Ops, SparseCore 0:
  10.5 36.7 all-gather.7
  58.0 114.7 all-gather.11
  174.4 113.5 all-gather.9
  290.2 22.0 all-gather.13
  314.7 38.8 all-gather.15
  355.9 38.7 all-gather.17
  560.6 209.7 reduce-scatter.8
  772.8 212.8 reduce-scatter.6
  989.1 43.3 reduce-scatter.12
  1035.9 76.8 reduce-scatter.14
  1116.3 76.8 reduce-scatter.16
  1196.5 65.4 reduce-scatter.10
  1264.7 134.2 all-reduce.20
where the time goes:
time: 1420 us; the launch traced here: 1410 us
  waiting for transfers between devices  915 us (64%)
  matrix products  258 us (18%)
  other arithmetic  78.9 us (6%)
  blocking collectives  73.7 us (5%)
  local copies, waits for them, and re-layouts  68.1 us (5%)
  between operations  18.3 us (1%)
    reduce_scatter x1, waiting for transfers between devices, shards(): lax.psum_scatter(grad_key_rows.reshape(row_count, row_len, features), 'se...  207 us
    reduce_scatter x1, waiting for transfers between devices, shards(): lax.psum_scatter(grad_value_rows.reshape(row_count, row_len, features), '...  179 us
    all_gather x1, waiting for transfers between devices, shards(): lax.all_gather(value_local, 'seq', axis=1, tiled=True)  106 us
    all_gather x1, waiting for transfers between devices, shards(): lax.all_gather(key_local, 'seq', axis=1, tiled=True)  92.8 us
    reduce_scatter x1, waiting for transfers between devices, shards(): lax.psum_scatter(g_reduce_weight, 'dp', scatter_dimension=0, tiled=True)  80.4 us
    reduce_scatter x1, waiting for transfers between devices, shards(): lax.psum_scatter(g_expand_weight, 'dp', scatter_dimension=0, tiled=True)  80.2 us
    psum x1, waiting for transfers between devices, shards(): lax.psum((every_shard[0], every_shard[1], every_shard[2], every_shard[3],...  74 us
    reduce_scatter x1, waiting for transfers between devices, shards(): lax.psum_scatter(g_joint_weight, 'dp', scatter_dimension=0, tiled=True)  68.9 us
  transfers between devices with their start and end apart: 13, of which 9 were waited for; matrix products, arithmetic and copies ran while one was open for 16% of the time, Pallas kernels for 0%

commit v1 on v0

--- a/solution.py
+++ b/solution.py
@@ -8,6 +8,32 @@
 keep_ratio_inverse = 1.0 / 0.9
 score_factor = 0.125
 norm_epsilon = 1e-06
+
+
+def meet_flows_by_axis(z_in, join_dim):
+    block_next = list(z_in.shape[1:])
+    block_next[join_dim] *= z_in.shape[0]
+    return jnp.moveaxis(z_in, 0, join_dim).reshape(block_next)
+
+
+def _name_node(patch, dev_axis):
+    low = lax.axis_index(dev_axis)
+    small = lax.axis_size(dev_axis)
+    h_now, side_arr = (small, low)
+    field_out, main = (patch[None], 1)
+    while main < h_now:
+        newest = lax.ppermute(field_out, dev_axis, [(c, c ^ main) for c in range(h_now)])
+        u_next = side_arr & main == 0
+        w2 = jnp.where(u_next, field_out, newest)
+        formed = jnp.where(u_next, newest, field_out)
+        field_out = jnp.concatenate([w2, formed])
+        main *= 2
+    return field_out
+
+
+def _launch_works(incoming_x, xx, array_dim=1):
+    earlier = _name_node(incoming_x, xx)
+    return meet_flows_by_axis(earlier, array_dim)
 
 
 def normalize(inputs, gain, shift_b):
@@ -142,7 +168,7 @@
     value_local = projected[:, 2 * features :].reshape(row_count, shard_len, features)
     key_rows, value_rows = (
         lax.all_gather(key_local, "seq", axis=1, tiled=True),
-        lax.all_gather(value_local, "seq", axis=1, tiled=True),
+        _launch_works(value_local, "seq"),
     )
     key_heads = key_rows.reshape(row_count, row_len, HEADS, HEAD)
     value_heads = value_rows.reshape(row_count, row_len, HEADS, HEAD)

time: 1420 us -> 1490 us (1.049)
  waiting for transfers between devices: 915 us -> 950 us
  local copies, waits for them, and re-layouts: 68.1 us -> 86.2 us
    ppermute x0 -> x2, waiting for transfers between devices: none -> 229 us  [_name_node(): lax.ppermute(field_out, dev_axis, [(c, c ^ main) for c in range(h_now)])]
    all_gather x1 -> x0, waiting for transfers between devices: 106 us -> none  [shards(): lax.all_gather(value_local, 'seq', axis=1, tiled=True)]
    all_gather x1, waiting for transfers between devices: 92.8 us -> 0.01 us  [shards(): lax.all_gather(key_local, 'seq', axis=1, tiled=True)]
    reduce_scatter x1, waiting for transfers between devices: 179 us -> 207 us  [shards(): lax.psum_scatter(grad_value_rows.reshape(row_count, row_len, features), '...]
    reduce_scatter x1, waiting for transfers between devices: 207 us -> 185 us  [shards(): lax.psum_scatter(grad_key_rows.reshape(row_count, row_len, features), 'se...]
  transfers between devices with their start and end apart: 13 -> 14, of which waited for: 9 -> 9; matrix products, arithmetic and copies ran while one was open for 16% -> 16% of each run, Pallas kernels for 0% -> 0%
where the time goes in v1:
time: 1490 us; the launch traced here: 1480 us
  waiting for transfers between devices  950 us (64%)
  matrix products  257 us (17%)
  local copies, waits for them, and re-layouts  86.2 us (6%)
  other arithmetic  86.1 us (6%)
  blocking collectives  73.2 us (5%)
  between operations  18.6 us (1%)
    ppermute x2, waiting for transfers between devices, _name_node(): lax.ppermute(field_out, dev_axis, [(c, c ^ main) for c in range(h_now)])  229 us
    reduce_scatter x1, waiting for transfers between devices, shards(): lax.psum_scatter(grad_value_rows.reshape(row_count, row_len, features), '...  207 us
    reduce_scatter x1, waiting for transfers between devices, shards(): lax.psum_scatter(grad_key_rows.reshape(row_count, row_len, features), 'se...  185 us
    reduce_scatter x1, waiting for transfers between devices, shards(): lax.psum_scatter(g_expand_weight, 'dp', scatter_dimension=0, tiled=True)  80.3 us
    reduce_scatter x1, waiting for transfers between devices, shards(): lax.psum_scatter(g_reduce_weight, 'dp', scatter_dimension=0, tiled=True)  80.2 us
    psum x1, waiting for transfers between devices, shards(): lax.psum((every_shard[0], every_shard[1], every_shard[2], every_shard[3],...  73.8 us
    reduce_scatter x1, waiting for transfers between devices, shards(): lax.psum_scatter(g_joint_weight, 'dp', scatter_dimension=0, tiled=True)  69 us
    dot_general x4, matrix products, matmul(): return jnp.dot(left, right, preferred_element_type=jnp.float32)  57.5 us
  transfers between devices with their start and end apart: 14, of which 9 were waited for; matrix products, arithmetic and copies ran while one was open for 16% of the time, Pallas kernels for 0%

profile of v1, /device:TPU:0, one launch (start us, length us, event | category | flops | bytes accessed | tf_op | source)
XLA Modules:
  0.0 1479.6 jit_solution(1962112909415131694)
XLA Ops:
  18.1 27.3 %all-reduce.18 = (bf16[768]{0:T(1024)(128)(2,1)S(1)}, bf16[768]{0:T(1024)(128)(2,1)S(1)}, bf16[1536]{0:T(1024)(128)(2,1)S(1)}, bf16[768]{0:T(1024)(128)(2,1)S(1)...) all-reduce(bf16[768]{0:T(1024)(128)(2,1)S(1)} %dynamic-update-slice, ...), channel_id=1, replica_groups=mesh['dp'=8,'seq'=4] {'dp'}, use_global_device_ids=true, to_apply=%add.1 | all-reduce | flops 6144 | bytes 24576
  62.9 108.5 %collective-permute-done = bf16[1,4,256,768]{3,2,1,0:T(8,128)(2,1)} collective-permute-done((bf16[1,4,256,768]{3,2,1,0:T(8,128)(2,1)S(1)}, bf16[1,4,256,768]{3,2,1,0:T(8,128)(2,1)}, u32[]{:S(2)}, u32[]{:S(2)}) %collective-permute-start) | collective-permute-done | bytes 1572896 | tf_op jit(solution)/shard_map/ppermute | solution.py:25
  199.5 120.9 %collective-permute-done.1 = bf16[2,4,256,768]{3,2,1,0:T(8,128)(2,1)} collective-permute-done((bf16[2,4,256,768]{3,2,1,0:T(8,128)(2,1)}, bf16[2,4,256,768]{3,2,1,0:T(8,128)(2,1)}, u32[]{:S(2)}, u32[]{:S(2)}) %collective-permute-start.1) | collective-permute-done | bytes 3145760 | tf_op jit(solution)/shard_map/ppermute | solution.py:25
  325.8 10.7 copy.74
  336.4 11.0 reshape_reshape.3
  356.2 52.8 %while.26 = (s32[]{:T(128)}, bf16[4,256,12,64]{1,3,2,0:T(8,128)(2,1)}, f32[4,12,256,1]{2,1,3,0:T(8,128)S(1)}, bf16[4,1024,12,64]{1,3,2,0:T(8,128)(2,1)}, s32[4,2...) while((s32[]{:T(128)}, ...), condition=%wide.region_6.7_spmd, body=%wide.region_3.6_spmd.sunk | while | flops 840365056 | bytes 42861672 | solution.py:175
  418.9 38.2 %multiply_convert_fusion.1 = (bf16[1024,3072]{1,0:T(8,128)(2,1)}, f32[1024,3072]{1,0:T(8,128)}, f32[1024,3072]{1,0:T(8,128)}) fusion(f32[3072]{0:T(1024)S(1)} %bitcast.251, bf16[768,3072]{1,0:T(8,128)(2,1)} %all-gather.13.cloned.1.call-done, f32[1024,768]{1,0:T(8,128)} %copy-done.2, f32[768]{0:T(1024)S(1)} %convert_element_type.152, ...), kind=kOutput, calls=%fused_computation.68 | convolution fusion | flops 5043388416 | bytes 39348224 | tf_op jit(solution)/shard_map/dot_general | solution.py:50
  457.1 17.5 %convert_reduce_fusion = (f32[3072]{0:T(1024)}, bf16[1024,3072]{1,0:T(8,128)(2,1)}) fusion(f32[1024,3072]{1,0:T(8,128)} %get-tuple-element.297, bf16[1024,768]{1,0:T(8,128)(2,1)S(1)} %copy-done.18, bf16[3072,768]{1,0:T(8,128)(2,1)} %all-gather.15.cloned.1.call-done, f32[1024,3072]{1,0:T(8,128)} %get-tuple-element.323, f32[3072]{0:T(1024)S(1)} %bitcast.252), kind=kOutput, calls=%fused_computation.66 | convolution fusion | flops 4885312512 | bytes 37773312 | tf_op jit(solution)/shard_map/dot_general | solution.py:60
  474.6 10.2 multiply_reduce_fusion.1
  497.6 125.1 %while.27 = (s32[]{:T(128)}, bf16[4,256,12,64]{1,3,2,0:T(8,128)(2,1)}, f32[4,1024,12,64]{1,3,2,0:T(8,128)}, f32[4,1024,12,64]{1,3,2,0:T(8,128)}, bf16[4,1024,12,...) while((s32[]{:T(128)}, ...), condition=%wide.region_14.15_spmd, body=%wide.region_12.14_spmd.sunk | while | flops 2061693952 | bytes 121487536 | solution.py:221
  563.5 8.8 multiply_reduce_fusion.5
  628.5 10.7 fusion.87
  639.4 9.9 fusion.98
  653.5 184.6 %reduce-scatter.7.cloned.1.call-done = f32[4,256,768]{1,2,0:T(8,128)} async-done(((f32[4,1024,768]{1,2,0:T(8,128)}), f32[4,256,768]{1,2,0:T(8,128)}) %reduce-scatter.7.cloned.1.call-update) | async-done | bytes 3145744 | tf_op jit(solution)/shard_map/reduce_scatter | solution.py:225
  846.5 206.9 %reduce-scatter.9.cloned.1.call-done = f32[4,256,768]{1,2,0:T(8,128)} async-done(((f32[4,1024,768]{1,2,0:T(8,128)}), f32[4,256,768]{1,2,0:T(8,128)}) %reduce-scatter.9.cloned.1.call-update) | async-done | bytes 3145744 | tf_op jit(solution)/shard_map/reduce_scatter | solution.py:231
  1061.7 9.8 fusion.84
  1075.4 24.8 %reduce-scatter.13.cloned.1.call-done = f32[96,768]{1,0:T(8,128)} async-done(((f32[768,768]{1,0:T(8,128)}), f32[96,768]{1,0:T(8,128)}) %reduce-scatter.13.cloned.1.call-update) | async-done | bytes 294928 | tf_op jit(solution)/shard_map/reduce_scatter | solution.py:260
  1100.1 80.3 %reduce-scatter.15.cloned.1.call-done = f32[96,3072]{1,0:T(8,128)} async-done(((f32[768,3072]{1,0:T(8,128)}), f32[96,3072]{1,0:T(8,128)}) %reduce-scatter.15.cloned.1.call-update) | async-done | bytes 1179664 | tf_op jit(solution)/shard_map/reduce_scatter | solution.py:264
  1180.5 80.2 %reduce-scatter.17.cloned.1.call-done = f32[384,768]{1,0:T(8,128)} async-done(((f32[3072,768]{1,0:T(8,128)}), f32[384,768]{1,0:T(8,128)}) %reduce-scatter.17.cloned.1.call-update) | async-done | bytes 1179664 | tf_op jit(solution)/shard_map/reduce_scatter | solution.py:266
  1260.7 69.0 %reduce-scatter.11.cloned.1.call-done = f32[96,2304]{1,0:T(8,128)} async-done(((f32[768,2304]{1,0:T(8,128)}), f32[96,2304]{1,0:T(8,128)}) %reduce-scatter.11.cloned.1.call-update) | async-done | bytes 884752 | tf_op jit(solution)/shard_map/reduce_scatter | solution.py:258
  1329.8 9.8 add_convert_fusion.2
  1348.8 25.1 %all-reduce.15 = (f32[768]{0:T(1024)S(1)}, f32[768]{0:T(1024)S(1)}, f32[1536]{0:T(1024)S(1)}, f32[768]{0:T(1024)S(1)}, f32[768]{0:T(1024)S(1)}, /*index=5*/f32[7...) all-reduce(f32[768]{0:T(1024)S(1)} %get-tuple-element.218, ...), channel_id=4, replica_groups=mesh['dp'=8,'seq'=4] {'dp'}, use_global_device_ids=true, to_apply=%region_20.21.clone | all-reduce | flops 9216 | bytes 73728
  1374.5 13.5 all-reduce.16
  1392.7 73.8 %all-reduce.21.cloned.1.call-done = (f32[96,2304]{1,0:T(8,128)}, f32[96,768]{1,0:T(8,128)}, f32[96,3072]{1,0:T(8,128)}, f32[384,768]{1,0:T(8,128)}) async-done(((f32[96,2304]{1,0:T(8,128)}, f32[96,768]{1,0:T(8,128)}, f32[96,3072]{1,0:T(8,128)}, f32[384,768]{1,0:T(8,128)}), (f32[96,2304]{1,0:T(8,128)}, f32[96,768]{1,0:T(8,128)}, f32[96,3072]{1,0:T(8,128)}, ...) | async-done | bytes 3538960 | tf_op jit(solution)/shard_map/psum | solution.py:282
  (339 shorter events, 309.2 us)
Async XLA Ops:
  7.2 39.9 %copy-start = (bf16[4,256,768]{2,1,0:T(8,128)(2,1)S(1)}, bf16[4,256,768]{2,1,0:T(8,128)(2,1)}, u32[]{:S(2)}) copy-start(bf16[4,256,768]{2,1,0:T(8,128)(2,1)} %param.20) | copy-start | bytes 4718596
  7.2 41.8 %all-gather.7.cloned.1.call-start = ((), (), s32[]{:S(2)}) async-start(), calls=%async_computation.6 | async-start | bytes 3981312 | tf_op jit(solution)/shard_map/all_gather | solution.py:149
  9.3 338.1 %all-gather.9.cloned.1.call-start = ((), (), s32[]{:S(2)}) async-start(), calls=%async_computation.7 | async-start | bytes 7864320 | tf_op jit(solution)/shard_map/all_gather | solution.py:170
  58.2 354.9 %all-gather.11.cloned.1.call-start = ((), (), s32[]{:S(2)}) async-start(), calls=%async_computation.8 | async-start | bytes 1327104 | tf_op jit(solution)/shard_map/all_gather | solution.py:151
  59.0 359.9 %all-gather.13.cloned.1.call-start = ((), (), s32[]{:S(2)}) async-start(), calls=%async_computation.9 | async-start | bytes 5308416 | tf_op jit(solution)/shard_map/all_gather | solution.py:184
  61.2 395.8 %all-gather.15.cloned.1.call-start = ((), (), s32[]{:S(2)}) async-start(), calls=%async_computation.10 | async-start | bytes 5308416 | tf_op jit(solution)/shard_map/all_gather | solution.py:186
  61.2 110.2 %collective-permute-start = (bf16[1,4,256,768]{3,2,1,0:T(8,128)(2,1)S(1)}, bf16[1,4,256,768]{3,2,1,0:T(8,128)(2,1)}, u32[]{:S(2)}, u32[]{:S(2)}) collective-permute-start(bf16[1,4,256,768]{3,2,1,0:T(8,128)(2,1)S(1)} %bitcast.225), channel_id=1, source_target_pairs={{0,1},{1,0},{2,3},{3,2},{4,5},{5,4},{6,7},{7,6},{8,9},{9,8},{10,11... | collective-permute-start | bytes 4718600 | tf_op jit(solution)/shard_map/ppermute | solution.py:25
  176.2 144.3 %collective-permute-start.1 = (bf16[2,4,256,768]{3,2,1,0:T(8,128)(2,1)}, bf16[2,4,256,768]{3,2,1,0:T(8,128)(2,1)}, u32[]{:S(2)}, u32[]{:S(2)}) collective-permute-start(bf16[2,4,256,768]{3,2,1,0:T(8,128)(2,1)} %pad_maximum_fusion.1), channel_id=1, source_target_pairs={{0,2},{1,3},{2,0},{3,1},{4,6},{5,7},{6,4},{7,5},{8,10},{9,11},{10,... | collective-permute-start | bytes 9437192 | tf_op jit(solution)/shard_map/ppermute | solution.py:25
  183.2 654.9 %reduce-scatter.7.cloned.1.call-start = ((), (), s32[]{:S(2)}) async-start(), calls=%async_computation.11 | async-start | bytes 15728640 | tf_op jit(solution)/shard_map/reduce_scatter | solution.py:225
  183.6 301.2 %copy-start.31 = (f32[768]{0:T(1024)}, f32[768]{0:T(1024)S(1)}, u32[]{:S(2)}) copy-start(f32[768]{0:T(1024)S(1)} %convert_element_type.150) | copy-start | bytes 9220
  183.6 235.2 %copy-start.39 = (f32[768]{0:T(1024)}, f32[768]{0:T(1024)S(1)}, u32[]{:S(2)}) copy-start(f32[768]{0:T(1024)S(1)} %convert_element_type.152) | copy-start | bytes 9220
  197.7 122.8 %copy-start.10 = (bf16[1,4,256,768]{3,2,1,0:T(8,128)(2,1)S(1)}, bf16[1,4,256,768]{3,2,1,0:T(8,128)(2,1)}, u32[]{:S(2)}) copy-start(bf16[1,4,256,768]{3,2,1,0:T(8,128)(2,1)} %copy-done.9) | copy-start | bytes 4718596
  197.7 122.8 %copy-start.12 = (bf16[1,4,256,768]{3,2,1,0:T(8,128)(2,1)S(1)}, bf16[1,4,256,768]{3,2,1,0:T(8,128)(2,1)}, u32[]{:S(2)}) copy-start(bf16[1,4,256,768]{3,2,1,0:T(8,128)(2,1)} %copy-done.11) | copy-start | bytes 4718596
  416.6 68.1 %copy-start.25 = (f32[1024]{0:T(1024)}, f32[1024]{0:T(1024)S(1)}, u32[]{:S(2)}) copy-start(f32[1024]{0:T(1024)S(1)} %broadcast_multiply_fusion) | copy-start | bytes 12292
  418.8 65.9 %copy-start.28 = (f32[1024]{0:T(1024)}, f32[1024]{0:T(1024)S(1)}, u32[]{:S(2)}) copy-start(f32[1024]{0:T(1024)S(1)} %fusion.81) | copy-start | bytes 12292
  622.7 430.7 %reduce-scatter.9.cloned.1.call-start = ((), (), s32[]{:S(2)}) async-start(), calls=%async_computation.12 | async-start | bytes 15728640 | tf_op jit(solution)/shard_map/reduce_scatter | solution.py:231
  623.5 476.6 %reduce-scatter.13.cloned.1.call-start = ((), (), s32[]{:S(2)}) async-start(), calls=%async_computation.14 | async-start | bytes 2654208 | tf_op jit(solution)/shard_map/reduce_scatter | solution.py:260
  628.4 552.0 %reduce-scatter.15.cloned.1.call-start = ((), (), s32[]{:S(2)}) async-start(), calls=%async_computation.15 | async-start | bytes 10616832 | tf_op jit(solution)/shard_map/reduce_scatter | solution.py:264
  639.3 621.4 %reduce-scatter.17.cloned.1.call-start = ((), (), s32[]{:S(2)}) async-start(), calls=%async_computation.16 | async-start | bytes 10616832 | tf_op jit(solution)/shard_map/reduce_scatter | solution.py:266
  649.3 680.5 %reduce-scatter.11.cloned.1.call-start = ((), (), s32[]{:S(2)}) async-start(), calls=%async_computation.13 | async-start | bytes 7962624 | tf_op jit(solution)/shard_map/reduce_scatter | solution.py:258
  1071.5 258.2 %copy-start.47 = (f32[1,2,4,128]{3,1,2,0:T(2,128)S(1)}, f32[1,2,4,128]{3,1,2,0:T(2,128)}, u32[]{:S(2)}) copy-start(f32[1,2,4,128]{3,1,2,0:T(2,128)} %copy-done.46) | copy-start | bytes 12292
  1071.6 395.0 %all-reduce.21.cloned.1.call-start = ((), (), s32[]{:S(2)}) async-start(), calls=%async_computation.17 | async-start | bytes 7077888 | tf_op jit(solution)/shard_map/psum | solution.py:282
  1345.6 42.4 %copy-start.8 = (bf16[4,256,768]{2,1,0:T(8,128)(2,1)S(1)}, bf16[4,256,768]{2,1,0:T(8,128)(2,1)}, u32[]{:S(2)}) copy-start(bf16[4,256,768]{2,1,0:T(8,128)(2,1)} %param.21) | copy-start | bytes 4718596
  1345.6 42.4 %copy-start.44 = (f32[1024]{0:T(1024)S(1)}, f32[1024]{0:T(1024)}, u32[]{:S(2)}) copy-start(f32[1024]{0:T(1024)} %copy-done.43) | copy-start | bytes 12292
  (53 other events, 266.8 us)
Sparse Core Ops, SparseCore 0:
  10.5 36.7 all-gather.6
  58.3 162.7 all-gather.8
  223.6 23.4 all-gather.10
  249.4 38.7 all-gather.12
  290.6 38.7 all-gather.14
  622.8 215.2 reduce-scatter.6
  840.4 212.8 reduce-scatter.8
  1056.7 43.3 reduce-scatter.12
  1103.6 76.7 reduce-scatter.14
  1183.8 76.8 reduce-scatter.16
  1264.2 65.4 reduce-scatter.10
  1332.2 134.2 all-reduce.20
